TPU v7x, 256 devices: a whole 4x4x8 slice. The times are simulated.
256 devices in a mesh: dp: 32 (over z, x_hi, core), slab: 8 (over y, x_lo).
Axes of the slice: x: 4 (x_hi: 2, x_lo: 2; x = x_hi * 2 + x_lo), y: 4, z: 8, core: 2. Of those that a mesh axis runs over, the one named last changes fastest.
Arguments:
- point_feats: bfloat16 [32, 128, 64, 128], P('dp', 'slab'), may hold values from -6 to 6
- point_coords: bfloat16 [32, 128, 3, 128], P('dp', 'slab'), may hold values from 0 to 1
- slot_block: int32 [32, 8, 8, 4], P('dp', 'slab'), may hold values from 0 to 15
- slot_cell: int32 [32, 8, 8, 4], P('dp', 'slab'), may hold values from 0 to 2047, as said below
- slot_count: int32 [32, 8, 8], P('dp', 'slab'), may hold values from 1 to 4, as said below
- cotangent: float32 [32, 16, 16, 16, 128], P('dp', 'slab'), may hold values from -6 to 6
- offset_map: float32 [64, 3], replicated, may hold values from -12 to 12
- offset_bias: float32 [64], replicated, may hold values from -4 to 4
- kernel_mix: bfloat16 [64, 64, 64], replicated, may hold values from -0.75 to 0.75
- lift_weight: bfloat16 [64, 64], replicated, may hold values from -0.75 to 0.75
Outputs:
- spectral_grad: float32 [64, 16, 16, 16, 128], P('dp', 'slab')
Inputs may be any that keep to these rules, and one draw needn't show every extreme that they name: `slot_cell`: cell row of a slot on its receiving slab index. `slot_count`: in every sample one receiving slab index, drawn from the seed, gets 4 live slots from every sending slab index.
All inputs are finite; a program needn't handle non-finite values.
Results may differ from a plain program's by a relative error of at most 0.0031.
Values may be sent and summed in bfloat16 or wider, within the bound.
A program may use at most 64 MiB of HBM per device.

v0:
```python
import math

import jax
import jax.numpy as jnp
import numpy as np
from jax import lax
from jax.experimental import pallas as pl
from jax.experimental.pallas import tpu as pltpu
from jax.sharding import PartitionSpec as P

F32 = jnp.float32
BF16 = jnp.bfloat16
NT = (((1,), (1,)), ((), ()))
VMEM_BYTES = 60 * 2**20


def split(x):
    hi = x.astype(BF16)
    return hi, (x - hi.astype(F32)).astype(BF16)


def dot3(a, b):
    ah, al = a
    bh, bl = b
    out = jnp.dot(ah, bh, preferred_element_type=F32)
    out = out + jnp.dot(al, bh, preferred_element_type=F32)
    return out + jnp.dot(ah, bl, preferred_element_type=F32)


def np_split(x):
    hi = np.asarray(x, np.float32).astype(BF16)
    lo = (np.asarray(x, np.float64) - hi.astype(np.float64)).astype(BF16)
    return hi, lo


def tables():
    z = np.arange(128)
    k = np.arange(16)
    turn = np.mod(z[:, None] * k[None, :], 128) * (2.0 * np.pi / 128)
    z_table = np.tile(np.concatenate([np.cos(turn), -np.sin(turn)], axis=1), (1, 8))
    z_hi, z_lo = np_split(z_table)
    signed = np.where(k < 8, k, k - 16)
    angle = np.mod(signed[:, None] * z[None, :], 128) * (2.0 * np.pi / 128)
    by_x = np.repeat(angle, 16, axis=0)
    by_y = np.tile(angle, (16, 1))
    xy = []
    for part in (np.cos(by_x), np.sin(by_x), np.cos(by_y), np.sin(by_y)):
        xy.append(np.concatenate(np_split(part), axis=1))
    return z_hi, z_lo, np.concatenate(xy, axis=0)


def terms_kernel(
    blk, cel, cnt, om, feats, coords, kmix, coef_ref, bias_ref, lift_ref, cot,
    out, tags, cot_out, mixed, mix, tab, base, coef, points, lifted, live, todo, seen,
):
    for b in range(16):
        seen[b] = 0

    def scan(n, carry):
        n_live, n_todo = carry
        slab = n // 4
        j = n - slab * 4
        is_live = j < cnt[0, slab]
        b = blk[j, slab]
        fresh = jnp.logical_and(is_live, seen[b] == 0)
        live[n_live] = n
        todo[n_todo] = b
        seen[b] = jnp.where(is_live, 1, seen[b])
        return n_live + is_live.astype(jnp.int32), n_todo + fresh.astype(jnp.int32)

    n_live, n_todo = lax.fori_loop(0, 32, scan, (jnp.int32(0), jnp.int32(0)))
    place = lax.broadcasted_iota(jnp.int32, (8, 256), 1) - 32 * lax.axis_index("slab")
    tag = jnp.zeros((8, 256), F32)
    for n in range(32):
        value = jnp.where(n % 4 < cnt[0, n // 4], (n // 4) * 2048 + cel[n % 4, n // 4], -1).astype(F32)
        tag = jnp.where(place == n, value, tag)
    tags[...] = tag
    for a in range(4):
        cot_out[a] = cot[a * 128 : (a + 1) * 128, :].T.astype(BF16)
    for h in range(32):
        both = jnp.concatenate([kmix[2 * h], kmix[2 * h + 1]], axis=1).astype(F32)
        mix[h * 128 : (h + 1) * 128, :] = both.T.astype(BF16)
    lifted[...] = jnp.zeros_like(lifted)
    pos_z = (lax.broadcasted_iota(jnp.int32, (128, 128), 0).astype(F32) + 0.5) * (1.0 / 128)

    def fill(h, carry):
        tab[h] = pos_z * om[2, h]
        return carry

    lax.fori_loop(0, 64, fill, 0)

    def mix_pair(i, carry):
        b0 = todo[2 * i]
        b1 = todo[jnp.minimum(2 * i + 1, n_todo - 1)]
        pair = jnp.concatenate([feats[b0], feats[b1]], axis=1)

        def rows(r, carry):
            start = pl.multiple_of(r * 512, 512)
            m = jnp.dot(mix[pl.ds(start, 512), :], pair, preferred_element_type=F32).astype(BF16)
            mixed[b0, pl.ds(start, 512), :] = m[:, :128]
            mixed[b1, pl.ds(start, 512), :] = m[:, 128:]
            return carry

        return lax.fori_loop(0, 8, rows, carry)

    lax.fori_loop(0, (n_todo + 1) // 2, mix_pair, 0)
    for c in range(3):
        coef[c] = jnp.broadcast_to(coef_ref[c : c + 1, :], (128, 64)).T
    coef[3] = jnp.broadcast_to(bias_ref[...], (128, 64)).T
    for c in range(3):
        by_block = coords[c].astype(F32)
        for b in range(16):
            points[b, c : c + 1, :] = by_block[b : b + 1, :]
    lift_v = lift_ref[...].astype(F32).T.astype(BF16)

    def slot(i, carry):
        n = live[i]
        slab = n // 4
        b = blk[n - slab * 4, slab]
        cell = cel[n - slab * 4, slab]
        x = slab * 16 + cell // 128
        y = lax.rem(cell, 128)
        pos_x = (x.astype(F32) + 0.5) * (1.0 / 128)
        pos_y = (y.astype(F32) + 0.5) * (1.0 / 128)
        coef_x, coef_y, coef_z = coef[0], coef[1], coef[2]
        point = coef_x * points[b, 0:1] + coef_y * points[b, 1:2] + coef_z * points[b, 2:3]
        base[...] = (coef_x * pos_x + coef_y * pos_y) + coef[3] - point
        ws, ms = [], []
        for h in range(64):
            w = (tab[h] + base[pl.ds(h, 1), :]).astype(BF16)
            ws.append(jnp.maximum(w, jnp.zeros_like(w)))
            ms.append(mixed[b, h * 64 : (h + 1) * 64, :])
        total = lax.dot_general(
            jnp.concatenate(ws, axis=1), jnp.concatenate(ms, axis=1), NT, preferred_element_type=F32
        )
        hi, lo = split(total.T * (1.0 / 128))
        pre = jnp.dot(lift_v, hi, preferred_element_type=F32) + jnp.dot(lift_v, lo, preferred_element_type=F32)
        lifted[pl.ds(pl.multiple_of(n * 64, 64), 64), :] = pre
        return carry

    lax.fori_loop(0, n_live, slot, 0)
    for e in range(64):
        out[e // 8, e % 8] = lifted[pl.ds(e, 32, stride=64), :].astype(BF16)


def lifted_terms(*args):
    sm = pl.BlockSpec(memory_space=pltpu.SMEM)
    vm = pl.BlockSpec(memory_space=pltpu.VMEM)
    return pl.pallas_call(
        terms_kernel,
        out_shape=(
            jax.ShapeDtypeStruct((8, 8, 32, 128), BF16),
            jax.ShapeDtypeStruct((8, 256), F32),
            jax.ShapeDtypeStruct((4, 128, 128), BF16),
        ),
        in_specs=[sm] * 4 + [vm] * 7,
        out_specs=(vm, vm, vm),
        scratch_shapes=[
            pltpu.VMEM((16, 4096, 128), BF16),
            pltpu.VMEM((4096, 64), BF16),
            pltpu.VMEM((64, 128, 128), F32),
            pltpu.VMEM((64, 128), F32),
            pltpu.VMEM((4, 64, 128), F32),
            pltpu.VMEM((16, 8, 128), F32),
            pltpu.VMEM((32 * 64, 128), F32),
            pltpu.SMEM((33,), jnp.int32),
            pltpu.SMEM((33,), jnp.int32),
            pltpu.SMEM((16,), jnp.int32),
        ],
        compiler_params=pltpu.CompilerParams(vmem_limit_bytes=VMEM_BYTES),
        name="slot_terms",
    )(*args)


def modes_value(tag_col, tag_row, terms, z_hi, z_lo, xy):
    lane = lax.broadcasted_iota(jnp.int32, (256, 256), 1)
    row = lax.broadcasted_iota(jnp.int32, (256, 256), 0)
    same = jnp.logical_and(tag_col == tag_row, tag_row >= 0)
    before = jnp.logical_and(same, lane < row)
    early = jnp.max(jnp.where(before, 1.0, 0.0), axis=1, keepdims=True)
    leader = jnp.where(tag_col[:, :1] >= 0, 1.0 - early, 0.0)
    sums = jnp.dot(jnp.where(same, 1.0, 0.0).astype(BF16), terms, preferred_element_type=F32)
    inner = math.sqrt(2.0 / math.pi) * (sums + 0.044715 * (sums * sums * sums))
    acts = (0.5 * leader) * (sums * (1.0 + jnp.tanh(inner)))
    z_lane = lax.broadcasted_iota(jnp.int32, (128, 256), 1) // 32
    zero = jnp.zeros((128, 256), BF16)
    zm = jnp.zeros((256, 256), F32)
    for e in range(8):
        pick = z_lane == e
        zm = zm + dot3(
            split(acts[:, e * 128 : (e + 1) * 128]),
            (jnp.where(pick, z_hi, zero), jnp.where(pick, z_lo, zero)),
        )
    imag_lane = (lane // 16) % 2 == 1
    swapped = jnp.where(imag_lane, pltpu.roll(zm, 16, 1), -pltpu.roll(zm, 240, 1))
    tag = jnp.maximum(tag_row, 0)
    pos = row % 128
    hot_x = jnp.where(pos == tag // 128, 1.0, 0.0).astype(BF16)
    hot_y = jnp.where(pos == tag % 128, 1.0, 0.0).astype(BF16)
    by_x = jnp.dot(xy[:512], hot_x, preferred_element_type=F32)
    by_y = jnp.dot(xy[512:], hot_y, preferred_element_type=F32)
    cos_x, sin_x, cos_y, sin_y = by_x[:256], by_x[256:], by_y[:256], by_y[256:]
    cos_part = cos_x * cos_y - sin_x * sin_y
    sin_part = -(sin_x * cos_y + cos_x * sin_y)
    out = dot3(split(cos_part), split(zm)) + dot3(split(sin_part), split(swapped))
    return out * (1.0 / math.sqrt(32768.0))


def swap_rows_runs(x):
    rows, lanes = x.shape
    row = lax.broadcasted_iota(jnp.int32, x.shape, 0) % 8
    run = (lax.broadcasted_iota(jnp.int32, x.shape, 1) % 128) // 16
    for step in (1, 2, 4):
        row_bit = (row // step) % 2
        run_bit = (run // step) % 2
        down = pltpu.roll(pltpu.roll(x, lanes - 16 * step, 1), step, 0)
        up = pltpu.roll(pltpu.roll(x, 16 * step, 1), rows - step, 0)
        x = jnp.where(row_bit == run_bit, x, jnp.where(row_bit == 1, down, up))
    return x


def exchange_kernel(
    terms, tags, cot, z_hi, z_lo, xy, out,
    terms_in, tags_in, cot_in, x_out, x_mid, x_in, pick, g_out, g_in, fold,
    t_send, t_recv, n_send, n_recv, c_send, c_recv, b_send, b_recv, y_send, y_recv, x_send, x_recv, g_send, g_recv,
):
    dp = lax.axis_index("dp")
    slab = lax.axis_index("slab")
    z = dp // 4
    part = dp - z * 4

    def copy_to(src, dst, send, recv, dp_to, slab_to):
        return pltpu.make_async_remote_copy(
            src_ref=src, dst_ref=dst, send_sem=send, recv_sem=recv,
            device_id=(dp_to, slab_to), device_id_type=pl.DeviceIdType.MESH,
        )

    def terms_copy(to):
        return copy_to(terms.at[to], terms_in.at[slab], t_send.at[to], t_recv.at[slab], dp, to)

    def tags_copy(to):
        return copy_to(tags, tags_in.at[slab], n_send.at[to], n_recv.at[slab], dp, to)

    def cot_copy(to):
        return copy_to(cot.at[to], cot_in.at[dp], c_send.at[to], c_recv.at[part], z * 4 + to, slab)

    def block_copy(k, ahead, step):
        src = lax.rem(z + ahead + 8, 8)
        block = cot_in.at[pl.ds(src * 4, 4)]
        to = lax.rem(z + step + 8, 8)
        return copy_to(block, block, b_send.at[k], b_recv.at[src], to * 4 + part, slab)

    block_sends = ((0, 0, 1), (1, 0, -1), (2, -1, 1), (3, 1, -1), (4, -2, 1), (5, 2, -1), (6, -3, 1))

    def wait_block(ahead):
        block_copy(0, ahead, 1).wait_recv()

    def slab_rows(at):
        return x_out.at[:, pl.ds(pl.multiple_of(at * 32, 32), 32)]

    def part_rows(at):
        return x_mid.at[at // 4, :, pl.ds(pl.multiple_of(lax.rem(at, 4) * 8, 8), 8)]

    def y_copy(to):
        return copy_to(slab_rows(to), x_mid.at[slab], y_send.at[to], y_recv.at[slab], dp, to)

    def x_copy(to):
        return copy_to(part_rows(to), x_in.at[dp], x_send.at[to], x_recv.at[dp], to, slab)

    def g_copy(to):
        return copy_to(g_out.at[to], g_in.at[part], g_send.at[to], g_recv.at[part], z * 4 + to, slab)

    own_terms = pltpu.make_async_copy(terms.at[slab], terms_in.at[slab], t_recv.at[slab])
    own_tags = pltpu.make_async_copy(tags, tags_in.at[slab], n_recv.at[slab])
    own_cot = pltpu.make_async_copy(cot.at[part], cot_in.at[dp], c_recv.at[part])
    own_y = pltpu.make_async_copy(slab_rows(slab), x_mid.at[slab], y_recv.at[slab])
    own_x = pltpu.make_async_copy(part_rows(dp), x_in.at[dp], x_recv.at[dp])

    def others(count, me, act):
        def step(i, carry):
            act(lax.rem(me + i, count))
            return carry

        lax.fori_loop(1, count, step, 0)

    barrier = pltpu.get_barrier_semaphore()

    def greet(dp_to, slab_to):
        pl.semaphore_signal(
            barrier, inc=1, device_id=(dp_to, slab_to), device_id_type=pl.DeviceIdType.MESH
        )

    others(8, slab, lambda to: greet(dp, to))
    others(32, dp, lambda to: greet(to, slab))
    pl.semaphore_wait(barrier, 7 + 31)

    own_terms.start()
    own_tags.start()
    own_cot.start()

    def start_slab(to):
        terms_copy(to).start()
        tags_copy(to).start()

    others(4, part, lambda to: cot_copy(to).start())
    others(8, slab, start_slab)
    own_cot.wait()

    def wait_cot(frm):
        copy_to(cot.at[frm], cot_in.at[z * 4 + frm], c_send.at[frm], c_recv.at[frm], z * 4 + frm, slab).wait_recv()

    others(4, part, wait_cot)

    def pass_block(k):
        if k > 1:
            wait_block(block_sends[k][1])
        block_copy(*block_sends[k]).start()

    pass_block(0)
    pass_block(1)

    own_terms.wait()
    own_tags.wait()

    def wait_slab(frm):
        copy_to(terms.at[frm], terms_in.at[frm], t_send.at[frm], t_recv.at[frm], dp, frm).wait_recv()
        copy_to(tags, tags_in.at[frm], n_send.at[frm], n_recv.at[frm], dp, frm).wait_recv()

    others(8, slab, wait_slab)
    pass_block(2)
    pass_block(3)
    t = jnp.concatenate(
        [jnp.concatenate([terms_in[r, e] for r in range(8)], axis=0) for e in range(8)], axis=1
    )
    tag_sum = tags_in[0]
    for r in range(1, 8):
        tag_sum = tag_sum + tags_in[r]
    row = jnp.broadcast_to(tag_sum[0:1, :], (256, 256))
    x = modes_value(row.T.astype(jnp.int32), row.astype(jnp.int32), t, z_hi[...], z_lo[...], xy[...])
    x = swap_rows_runs(x)
    x_out[0] = x[:, :128]
    x_out[1] = x[:, 128:]

    own_y.start()
    others(8, slab, lambda to: y_copy(to).start())
    pass_block(4)
    pass_block(5)

    def pass_on(frm):
        for a in range(4):
            to = frm * 4 + a

            @pl.when(to == dp)
            def _():
                own_x.start()

            @pl.when(to != dp)
            def _():
                x_copy(to).start()

    own_y.wait()
    pass_on(slab)

    def relay(frm):
        copy_to(slab_rows(0), x_mid.at[frm], y_send.at[frm], y_recv.at[frm], dp, frm).wait_recv()
        pass_on(frm)

    others(8, slab, relay)
    pass_block(6)
    for ahead in (3, 4):
        wait_block(ahead)

    def wait_x(frm):
        copy_to(part_rows(0), x_in.at[frm], x_send.at[frm], x_recv.at[frm], frm, slab).wait_recv()

    own_x.wait()
    others(32, dp, wait_x)

    def channels(to):
        both = x_in[:, to // 2]
        pick[...] = jnp.where(lax.rem(to, 2) == 1, pltpu.roll(both, 4, 1), both)
        for o in range(4):
            low = pl.ds(o * 16, 16)
            high = pl.ds(64 + o * 16, 16)

            def sample(s, acc):
                g_low = cot_in[s, low, :].astype(F32)
                g_high = cot_in[s, high, :].astype(F32)
                new = []
                for q in range(4):
                    xq = pick[s, q : q + 1, :]
                    new.append(acc[2 * q] + xq * g_low)
                    new.append(acc[2 * q + 1] + xq * g_high)
                return tuple(new)

            acc = lax.fori_loop(0, 32, sample, tuple(jnp.zeros((16, 128), F32) for _ in range(8)), unroll=4)
            for i in range(2):
                re_low, re_high, im_low, im_high = acc[4 * i : 4 * i + 4]
                fold[i, low, :] = re_low + im_high
                fold[i, high, :] = re_high - im_low
        for i in range(2):
            g_out[to, i] = fold[i].T.astype(BF16)

    def one(k, carry):
        other = (1 - part // 2) * 2 + k
        here = (part // 2) * 2 + lax.rem(part + k + 1, 2)
        to = jnp.where(k < 2, other, here)
        channels(to)

        @pl.when(k < 3)
        def _():
            g_copy(to).start()

        return carry

    lax.fori_loop(0, 4, one, 0)
    out[0, part] = g_out[part, 0]
    out[1, part] = g_out[part, 1]

    def take(frm):
        copy_to(g_out.at[frm], g_in.at[frm], g_send.at[frm], g_recv.at[frm], z * 4 + frm, slab).wait_recv()
        out[0, frm] = g_in[frm, 0]
        out[1, frm] = g_in[frm, 1]

    others(4, part, take)

    def sent_slab(to):
        terms_copy(to).wait_send()
        tags_copy(to).wait_send()

    others(8, slab, sent_slab)
    others(4, part, lambda to: cot_copy(to).wait_send())
    for k in range(7):
        block_copy(*block_sends[k]).wait_send()

    others(8, slab, lambda to: y_copy(to).wait_send())
    others(32, dp, lambda to: x_copy(to).wait_send())
    others(4, part, lambda to: g_copy(to).wait_send())


def exchange(terms, tags, cot):
    z_hi, z_lo, xy = (jnp.asarray(t) for t in tables())
    vm = pl.BlockSpec(memory_space=pltpu.VMEM)
    dma = pltpu.SemaphoreType.DMA
    return pl.pallas_call(
        exchange_kernel,
        out_shape=jax.ShapeDtypeStruct((2, 4, 128, 128), BF16),
        in_specs=[vm] * 6,
        out_specs=vm,
        scratch_shapes=[
            pltpu.VMEM((8, 8, 32, 128), BF16),
            pltpu.VMEM((8, 8, 256), F32),
            pltpu.VMEM((32, 128, 128), BF16),
            pltpu.VMEM((2, 256, 128), F32),
            pltpu.VMEM((8, 2, 32, 128), F32),
            pltpu.VMEM((32, 2, 8, 128), F32),
            pltpu.VMEM((32, 8, 128), F32),
            pltpu.VMEM((4, 2, 128, 128), BF16),
            pltpu.VMEM((4, 2, 128, 128), BF16),
            pltpu.VMEM((2, 128, 128), F32),
            dma((8,)), dma((8,)), dma((8,)), dma((8,)), dma((4,)), dma((4,)), dma((8,)), dma((8,)),
            dma((8,)), dma((8,)), dma((32,)), dma((32,)), dma((4,)), dma((4,)),
        ],
        compiler_params=pltpu.CompilerParams(
            vmem_limit_bytes=VMEM_BYTES, collective_id=0, has_side_effects=True
        ),
        name="exchange",
    )(terms, tags, cot, z_hi, z_lo, xy)


def per_device(
    point_feats, point_coords, slot_block, slot_cell, slot_count, cotangent,
    offset_map, offset_bias, kernel_mix, lift_weight,
):
    terms, tags, cot = lifted_terms(
        slot_block[0, 0].T, slot_cell[0, 0].T, slot_count[0], offset_map.T,
        point_feats[0], point_coords[0].transpose(1, 0, 2), kernel_mix, offset_map.T, offset_bias[None, :], lift_weight,
        cotangent.reshape(512, 128),
    )
    grad = exchange(terms, tags, cot)
    return grad.astype(F32).reshape(2, 2, 16, 16, 128)


def solution(mesh):
    placed = (
        P("dp", "slab", None, None), P("dp", "slab", None, None), P("dp", "slab", None, None),
        P("dp", "slab", None, None), P("dp", "slab", None), P("dp", "slab", None, None, None),
        P(), P(), P(), P(),
    )
    return jax.shard_map(
        per_device,
        mesh=mesh,
        in_specs=placed,
        out_specs=P("dp", "slab", None, None, None),
        check_vma=False,
    )
```

profile of v0, /device:TPU:3, one launch (start us, length us, event | category | flops | bytes accessed | tf_op | source)
XLA Modules:
  0.0 84.6 jit_solution(3598121766980626869)
XLA Ops:
  0.0 28.7 %slot_terms.1 = (bf16[8,8,32,128]{3,2,1,0:T(8,128)(2,1)}, f32[8,256]{1,0:T(8,128)}, bf16[4,128,128]{2,1,0:T(8,128)(2,1)}) custom-call(s32[4,8]{1,0:T(4,128)} %bitcast.22, s32[4,8]{1,0:T(4,128)} %bitcast.23, s32[1,8]{1,0:T(1,128)} %bitcast.24, f32[3,64]{1,0:T(4,128)} %bitcast.20, bf16[16,64,128]{2,1,0:T(8,128)(2,1)} %bitcast.17, ...), custom_call_target="tpu_custom_call" | custom-call | tf_op jit(solution)/shard_map/slot_terms/pallas_call | solution.py:149
  28.7 54.1 %exchange.1 = bf16[2,4,128,128]{3,2,1,0:T(8,128)(2,1)} custom-call(bf16[8,8,32,128]{3,2,1,0:T(8,128)(2,1)} %get-tuple-element.8.terms, f32[8,256]{1,0:T(8,128)} %get-tuple-element.9.tags, bf16[4,128,128]{2,1,0:T(8,128)(2,1)} %get-tuple-element.10.cot, bf16[128,256]{1,0:T(8,128)(2,1)} %constant.6.clone.z_hi, bf16[128,256]{1,0:T(8,128)(2,1)} %constant.7.clone.z_lo, ...), custom_call_target="tpu_custom_call" | custom-call | tf_op jit(solution)/shard_map/exchange/pallas_call | solution.py:445
  82.8 1.8 %convert.1 = f32[2,2,16,16,128]{4,3,2,1,0:T(8,128)} convert(bf16[2,2,16,16,128]{4,3,2,1,0:T(8,128)(2,1)} %bitcast.16) | non-fusion elementwise | flops 131072 | bytes 786432 | tf_op jit(solution)/shard_map/reshape | solution.py:481
where the time goes:
time: 83.8 us; the launch traced here: 84.6 us
  Pallas kernels  82.8 us (99%)
  other arithmetic  1.78 us (2%)
    pallas_call x1, Pallas kernels, exchange(): pl.pallas_call(exchange_kernel, out_shape=jax.ShapeDtypeStruct((2, 4, 128...  54.1 us
    pallas_call x1, Pallas kernels, lifted_terms(): pl.pallas_call(terms_kernel, out_shape=(jax.ShapeDtypeStruct((8, 8, 32, 1...  28.7 us
    reshape x1, other arithmetic, per_device(): return grad.astype(F32).reshape(2, 2, 16, 16, 128)  1.78 us

commit v1 on v0

--- a/solution.py
+++ b/solution.py
@@ -51,7 +51,7 @@
 
 def terms_kernel(
     blk, cel, cnt, om, feats, coords, kmix, coef_ref, bias_ref, lift_ref, cot,
-    out, tags, cot_out, mixed, mix, tab, base, coef, points, lifted, live, todo, seen,
+    out, tags, cot_out, mixed, mix, tab, base, coef, points, sums, lifted, live, todo, seen,
 ):
     for b in range(16):
         seen[b] = 0
@@ -95,13 +95,13 @@
         pair = jnp.concatenate([feats[b0], feats[b1]], axis=1)
 
         def rows(r, carry):
-            start = pl.multiple_of(r * 512, 512)
-            m = jnp.dot(mix[pl.ds(start, 512), :], pair, preferred_element_type=F32).astype(BF16)
-            mixed[b0, pl.ds(start, 512), :] = m[:, :128]
-            mixed[b1, pl.ds(start, 512), :] = m[:, 128:]
+            start = pl.multiple_of(r * 2048, 2048)
+            m = jnp.dot(mix[pl.ds(start, 2048), :], pair, preferred_element_type=F32).astype(BF16)
+            mixed[b0, pl.ds(start, 2048), :] = m[:, :128]
+            mixed[b1, pl.ds(start, 2048), :] = m[:, 128:]
             return carry
 
-        return lax.fori_loop(0, 8, rows, carry)
+        return lax.fori_loop(0, 2, rows, carry)
 
     lax.fori_loop(0, (n_todo + 1) // 2, mix_pair, 0)
     for c in range(3):
@@ -133,12 +133,20 @@
         total = lax.dot_general(
             jnp.concatenate(ws, axis=1), jnp.concatenate(ms, axis=1), NT, preferred_element_type=F32
         )
-        hi, lo = split(total.T * (1.0 / 128))
-        pre = jnp.dot(lift_v, hi, preferred_element_type=F32) + jnp.dot(lift_v, lo, preferred_element_type=F32)
-        lifted[pl.ds(pl.multiple_of(n * 64, 64), 64), :] = pre
+        sums[i] = total
         return carry
 
     lax.fori_loop(0, n_live, slot, 0)
+
+    def lift_four(g, carry):
+        for u in range(4):
+            i = jnp.minimum(4 * g + u, n_live - 1)
+            hi, lo = split(sums[i].T * (1.0 / 128))
+            pre = jnp.dot(lift_v, hi, preferred_element_type=F32) + jnp.dot(lift_v, lo, preferred_element_type=F32)
+            lifted[pl.ds(pl.multiple_of(live[i] * 64, 64), 64), :] = pre
+        return carry
+
+    lax.fori_loop(0, (n_live + 3) // 4, lift_four, 0)
     for e in range(64):
         out[e // 8, e % 8] = lifted[pl.ds(e, 32, stride=64), :].astype(BF16)
 
@@ -162,6 +170,7 @@
             pltpu.VMEM((64, 128), F32),
             pltpu.VMEM((4, 64, 128), F32),
             pltpu.VMEM((16, 8, 128), F32),
+            pltpu.VMEM((32, 128, 64), F32),
             pltpu.VMEM((32 * 64, 128), F32),
             pltpu.SMEM((33,), jnp.int32),
             pltpu.SMEM((33,), jnp.int32),

time: 83.8 us -> 73.9 us (0.88); the launches traced: 84.6 us -> 72.9 us
  Pallas kernels: 82.8 us -> 71.1 us
    pallas_call x1, Pallas kernels: 28.7 us -> 20.8 us  [lifted_terms(): pl.pallas_call(terms_kernel, out_shape=(jax.ShapeDtypeStruct((8, 8, 32, 1...]
    pallas_call x1, Pallas kernels: 54.1 us -> 50.3 us  [exchange(): pl.pallas_call(exchange_kernel, out_shape=jax.ShapeDtypeStruct((2, 4, 128...]
where the time goes in v1:
time: 73.9 us; the launch traced here: 72.9 us
  Pallas kernels  71.1 us (96%)
  other arithmetic  1.78 us (2%)
    pallas_call x1, Pallas kernels, exchange(): pl.pallas_call(exchange_kernel, out_shape=jax.ShapeDtypeStruct((2, 4, 128...  50.3 us
    pallas_call x1, Pallas kernels, lifted_terms(): pl.pallas_call(terms_kernel, out_shape=(jax.ShapeDtypeStruct((8, 8, 32, 1...  20.8 us
    reshape x1, other arithmetic, per_device(): return grad.astype(F32).reshape(2, 2, 16, 16, 128)  1.78 us

profile of v1, /device:TPU:3, one launch (start us, length us, event | category | flops | bytes accessed | tf_op | source)
XLA Modules:
  0.0 72.9 jit_solution(8706606583205240998)
XLA Ops:
  0.0 20.8 %slot_terms.1 = (bf16[8,8,32,128]{3,2,1,0:T(8,128)(2,1)}, f32[8,256]{1,0:T(8,128)}, bf16[4,128,128]{2,1,0:T(8,128)(2,1)}) custom-call(s32[4,8]{1,0:T(4,128)} %bitcast.22, s32[4,8]{1,0:T(4,128)} %bitcast.23, s32[1,8]{1,0:T(1,128)} %bitcast.24, f32[3,64]{1,0:T(4,128)} %bitcast.20, bf16[16,64,128]{2,1,0:T(8,128)(2,1)} %bitcast.17, ...), custom_call_target="tpu_custom_call" | custom-call | tf_op jit(solution)/shard_map/slot_terms/pallas_call | solution.py:157
  20.8 50.3 %exchange.1 = bf16[2,4,128,128]{3,2,1,0:T(8,128)(2,1)} custom-call(bf16[8,8,32,128]{3,2,1,0:T(8,128)(2,1)} %get-tuple-element.8.terms, f32[8,256]{1,0:T(8,128)} %get-tuple-element.9.tags, bf16[4,128,128]{2,1,0:T(8,128)(2,1)} %get-tuple-element.10.cot, bf16[128,256]{1,0:T(8,128)(2,1)} %constant.6.clone.z_hi, bf16[128,256]{1,0:T(8,128)(2,1)} %constant.7.clone.z_lo, ...), custom_call_target="tpu_custom_call" | custom-call | tf_op jit(solution)/shard_map/exchange/pallas_call | solution.py:454
  71.1 1.8 %convert.1 = f32[2,2,16,16,128]{4,3,2,1,0:T(8,128)} convert(bf16[2,2,16,16,128]{4,3,2,1,0:T(8,128)(2,1)} %bitcast.16) | non-fusion elementwise | flops 131072 | bytes 786432 | tf_op jit(solution)/shard_map/reshape | solution.py:490

commit v2 on v1

--- a/solution.py
+++ b/solution.py
@@ -83,11 +83,12 @@
     lifted[...] = jnp.zeros_like(lifted)
     pos_z = (lax.broadcasted_iota(jnp.int32, (128, 128), 0).astype(F32) + 0.5) * (1.0 / 128)
 
-    def fill(h, carry):
-        tab[h] = pos_z * om[2, h]
+    def fill(g, carry):
+        for u in range(8):
+            tab[8 * g + u] = pos_z * om[2, 8 * g + u]
         return carry
 
-    lax.fori_loop(0, 64, fill, 0)
+    lax.fori_loop(0, 8, fill, 0)
 
     def mix_pair(i, carry):
         b0 = todo[2 * i]
@@ -95,13 +96,13 @@
         pair = jnp.concatenate([feats[b0], feats[b1]], axis=1)
 
         def rows(r, carry):
-            start = pl.multiple_of(r * 2048, 2048)
-            m = jnp.dot(mix[pl.ds(start, 2048), :], pair, preferred_element_type=F32).astype(BF16)
-            mixed[b0, pl.ds(start, 2048), :] = m[:, :128]
-            mixed[b1, pl.ds(start, 2048), :] = m[:, 128:]
+            start = pl.multiple_of(r * 4096, 4096)
+            m = jnp.dot(mix[pl.ds(start, 4096), :], pair, preferred_element_type=F32).astype(BF16)
+            mixed[b0, pl.ds(start, 4096), :] = m[:, :128]
+            mixed[b1, pl.ds(start, 4096), :] = m[:, 128:]
             return carry
 
-        return lax.fori_loop(0, 2, rows, carry)
+        return lax.fori_loop(0, 1, rows, carry)
 
     lax.fori_loop(0, (n_todo + 1) // 2, mix_pair, 0)
     for c in range(3):
@@ -402,7 +403,7 @@
                     new.append(acc[2 * q + 1] + xq * g_high)
                 return tuple(new)
 
-            acc = lax.fori_loop(0, 32, sample, tuple(jnp.zeros((16, 128), F32) for _ in range(8)), unroll=4)
+            acc = lax.fori_loop(0, 32, sample, tuple(jnp.zeros((16, 128), F32) for _ in range(8)), unroll=8)
             for i in range(2):
                 re_low, re_high, im_low, im_high = acc[4 * i : 4 * i + 4]
                 fold[i, low, :] = re_low + im_high

time: 73.9 us -> 72.9 us (0.986); the launches traced: 72.9 us -> 72.9 us
    pallas_call x1, Pallas kernels: 20.8 us -> 19.1 us  [lifted_terms(): pl.pallas_call(terms_kernel, out_shape=(jax.ShapeDtypeStruct((8, 8, 32, 1...]
    pallas_call x1, Pallas kernels: 50.3 us -> 52 us  [exchange(): pl.pallas_call(exchange_kernel, out_shape=jax.ShapeDtypeStruct((2, 4, 128...]
where the time goes in v2:
time: 72.9 us
  Pallas kernels  71.1 us (98%)
  other arithmetic  1.78 us (2%)
    pallas_call x1, Pallas kernels, exchange(): pl.pallas_call(exchange_kernel, out_shape=jax.ShapeDtypeStruct((2, 4, 128...  52 us
    pallas_call x1, Pallas kernels, lifted_terms(): pl.pallas_call(terms_kernel, out_shape=(jax.ShapeDtypeStruct((8, 8, 32, 1...  19.1 us
    reshape x1, other arithmetic, per_device(): return grad.astype(F32).reshape(2, 2, 16, 16, 128)  1.78 us

profile of v2, /device:TPU:3, one launch (start us, length us, event | category | flops | bytes accessed | tf_op | source)
XLA Modules:
  0.0 72.9 jit_solution(13610078973090735015)
XLA Ops:
  0.0 19.1 %slot_terms.1 = (bf16[8,8,32,128]{3,2,1,0:T(8,128)(2,1)}, f32[8,256]{1,0:T(8,128)}, bf16[4,128,128]{2,1,0:T(8,128)(2,1)}) custom-call(s32[4,8]{1,0:T(4,128)} %bitcast.22, s32[4,8]{1,0:T(4,128)} %bitcast.23, s32[1,8]{1,0:T(1,128)} %bitcast.24, f32[3,64]{1,0:T(4,128)} %bitcast.20, bf16[16,64,128]{2,1,0:T(8,128)(2,1)} %bitcast.17, ...), custom_call_target="tpu_custom_call" | custom-call | tf_op jit(solution)/shard_map/slot_terms/pallas_call | solution.py:158
  19.1 52.0 %exchange.1 = bf16[2,4,128,128]{3,2,1,0:T(8,128)(2,1)} custom-call(bf16[8,8,32,128]{3,2,1,0:T(8,128)(2,1)} %get-tuple-element.8.terms, f32[8,256]{1,0:T(8,128)} %get-tuple-element.9.tags, bf16[4,128,128]{2,1,0:T(8,128)(2,1)} %get-tuple-element.10.cot, bf16[128,256]{1,0:T(8,128)(2,1)} %constant.6.clone.z_hi, bf16[128,256]{1,0:T(8,128)(2,1)} %constant.7.clone.z_lo, ...), custom_call_target="tpu_custom_call" | custom-call | tf_op jit(solution)/shard_map/exchange/pallas_call | solution.py:455
  71.1 1.8 %convert.1 = f32[2,2,16,16,128]{4,3,2,1,0:T(8,128)} convert(bf16[2,2,16,16,128]{4,3,2,1,0:T(8,128)(2,1)} %bitcast.16) | non-fusion elementwise | flops 131072 | bytes 786432 | tf_op jit(solution)/shard_map/reshape | solution.py:491
